TPU v7x, 256 devices: a whole 4x4x8 slice. The times are simulated.
256 devices in a mesh: env: 4 (over x_lo, core), tm: 64 (over x_hi, z, y).
Axes of the slice: x: 4 (x_hi: 2, x_lo: 2; x = x_hi * 2 + x_lo), y: 4, z: 8, core: 2. Of those that a mesh axis runs over, the one named last changes fastest.
Arguments:
- hidden: bfloat16 [4, 64, 256, 1024], P('env', 'tm'), may hold values from -6 to 6
- done_step: int32 [4, 64], P('env', 'tm'), may hold values from 0 to 255
- alive: int32 [4, 64, 256], P('env', None, 'tm'), may hold values 0 or 1
- targets: float32 [4, 64, 256], P('env', None, 'tm'), may hold values from -6 to 6
- gain_t: float32 [1024], replicated, may hold values from 0.25 to 1.75
- w_qkv_t: bfloat16 [1024, 3072], replicated, may hold values from -5 to 5
- w_out_t: bfloat16 [1024, 1024], replicated, may hold values from -0.1875 to 0.1875
- gain_a: float32 [1024], replicated, may hold values from 0.25 to 1.75
- w_qkv_a: bfloat16 [1024, 3072], P('tm'), may hold values from -5 to 5
- w_out_a: bfloat16 [1024, 1024], P('tm'), may hold values from -0.1875 to 0.1875
- w_value: float32 [1024], replicated, may hold values from -0.1875 to 0.1875
Outputs:
- values: float32 [4, 64, 256], P('env', None, 'tm')
- input_grad: bfloat16 [4, 64, 256, 1024], P('env', 'tm')
- qkv_grad: float32 [1024, 3072], P('tm')
- out_grad: float32 [1024, 1024], P('tm')
Inputs may be any that keep to these rules, and one draw needn't show every extreme that they name: `done_step`: the last step of an agent's first episode in the window; later steps form a new episode.
All inputs are finite; a program needn't handle non-finite values. No bound on the sum of `alive` on one device may be relied on, other than what follows from the above.
Results may differ from a plain program's by a relative error of at most 0.02.
Values may be sent and summed in bfloat16 or wider, within the bound.
A program may use at most 128 MiB of HBM per device.

v0:
```python
import math
import jax
import jax.numpy as jnp
from jax import lax
from jax.sharding import PartitionSpec as P

HEADS = 8
HI = lax.Precision.HIGHEST


def norm_scale(rows, gain):
    return rows * lax.rsqrt(jnp.mean(rows * rows, axis=-1, keepdims=True) + 1e-06) * gain


def attend(qkv, allowed, head_count):
    width = qkv.shape[-1] // 3
    size = width // head_count
    shape = qkv.shape[:-1] + (head_count, size)
    queries = qkv[..., :width].reshape(shape)
    key_rows = qkv[..., width : 2 * width].reshape(shape)
    value_rows = qkv[..., 2 * width :].reshape(shape)
    scores = jnp.einsum("qhe,khe->hqk", queries, key_rows, preferred_element_type=jnp.float32)
    scores = jnp.where(allowed[None], scores / math.sqrt(size), -1e30)
    row_max = jnp.max(scores, axis=-1, keepdims=True)
    weights = jnp.exp(scores - row_max)
    probs = (weights / jnp.sum(weights, axis=-1, keepdims=True)).astype(jnp.bfloat16)
    mixed = jnp.einsum("hqk,khe->qhe", probs, value_rows, preferred_element_type=jnp.float32)
    return mixed.reshape(qkv.shape[:-1] + (width,))


def temporal_block(rows, done, gain, w_qkv, w_out, head_count):
    length, width = rows.shape
    rows_f = rows.astype(jnp.float32)
    normed = norm_scale(rows_f, gain).astype(jnp.bfloat16)
    qkv = jnp.dot(normed, w_qkv, preferred_element_type=jnp.float32).astype(jnp.bfloat16)
    positions = jnp.arange(length, dtype=jnp.int32)
    later = positions > done
    allowed = (positions[:, None] >= positions[None, :]) & (later[:, None] == later[None, :])
    mixed = attend(qkv, allowed, head_count).astype(jnp.bfloat16)
    added = jnp.dot(mixed, w_out, preferred_element_type=jnp.float32)
    return (rows_f + added).astype(jnp.bfloat16)


def left_product(left, right):
    return lax.dot_general(
        left, right, (((0,), (0,)), ((), ())), preferred_element_type=jnp.float32
    )


def agent_step(lifted, alive_rows, target_rows, gain, w_qk, z, w_value, head_count):
    agent_count, step_count, width = lifted.shape
    size = width // head_count
    lifted_f = lifted.astype(jnp.float32)
    normed_f, norm_pull = jax.vjp(lambda rows: norm_scale(rows, gain), lifted_f)
    normed = normed_f.astype(jnp.bfloat16).reshape(-1, width)
    qk = jnp.dot(normed, w_qk, preferred_element_type=jnp.float32).astype(jnp.bfloat16)
    qk = qk.reshape(agent_count, step_count, 2, head_count, size)
    q, k = (qk[:, :, 0], qk[:, :, 1])
    s = jnp.dot(normed.astype(jnp.float32), z, precision=HI)
    s = s.reshape(agent_count, step_count, head_count).transpose(1, 2, 0)
    living = alive_rows.T == 1
    allowed = living[:, None, :] | jnp.eye(agent_count, dtype=bool)[None]
    scores = jnp.einsum("qbhe,kbhe->bhqk", q, k, preferred_element_type=jnp.float32)
    scores = jnp.where(allowed[:, None], scores / math.sqrt(size), -1e30)
    weights = jnp.exp(scores - jnp.max(scores, axis=-1, keepdims=True))
    probs = weights / jnp.sum(weights, axis=-1, keepdims=True)
    pv = jnp.sum(probs * s[:, :, None, :], axis=-1)
    predicted = jnp.sum(lifted_f * w_value, axis=-1) + jnp.sum(pv, axis=1).T
    err = 32.0 * alive_rows.astype(jnp.float32) * (predicted - target_rows)
    weighted = probs * err.T[:, None, :, None]
    t = jnp.sum(weighted, axis=2)
    ds = weighted * (s[:, :, None, :] - pv[..., None]) * (1.0 / math.sqrt(size))
    ds = ds.astype(jnp.bfloat16)
    dq = jnp.einsum("bhqk,kbhe->qbhe", ds, k, preferred_element_type=jnp.float32)
    dk = jnp.einsum("bhqk,qbhe->kbhe", ds, q, preferred_element_type=jnp.float32)
    dqk = jnp.stack([dq, dk], axis=2).astype(jnp.bfloat16).reshape(-1, 2 * width)
    t = t.transpose(2, 0, 1).reshape(-1, head_count)
    grad_normed = jnp.dot(dqk, w_qk.T, preferred_element_type=jnp.float32)
    grad_normed = grad_normed + jnp.dot(t, z.T, precision=HI)
    grad_top = err[..., None] * w_value
    grad_lifted = grad_top + norm_pull(grad_normed.reshape(agent_count, step_count, width))[0]
    return (predicted, grad_lifted.astype(jnp.bfloat16), normed, dqk, t)


def per_device(
    hidden, done_step, alive, targets, gain_t, w_qkv_t, w_out_t, gain_a, w_qkv_a, w_out_a, w_value
):
    width = hidden.shape[-1]
    size = width // HEADS
    local_rows = hidden[0, 0]
    done = done_step[0, 0]
    v = lax.all_gather(
        jnp.sum(w_out_a.astype(jnp.float32) * w_value, axis=1), "tm", axis=0, tiled=True
    )
    w_v = w_qkv_a[:, 2 * width :].astype(jnp.float32)
    z = jnp.sum((w_v * v).reshape(-1, HEADS, size), axis=-1)
    z = lax.all_gather(z, "tm", axis=0, tiled=True)
    w_qk = lax.all_gather(w_qkv_a[:, : 2 * width], "tm", axis=0, tiled=True)
    first, pull = jax.vjp(
        lambda rows: temporal_block(rows, done, gain_t, w_qkv_t, w_out_t, HEADS), local_rows
    )
    lifted = lax.all_to_all(first[None], "tm", split_axis=1, concat_axis=0, tiled=True)
    predicted, grad_lifted, normed, dqk, t = agent_step(
        lifted, alive[0], targets[0], gain_a, w_qk, z, w_value, HEADS
    )
    returned = lax.all_to_all(grad_lifted, "tm", split_axis=0, concat_axis=1, tiled=True)
    terms = left_product(normed, dqk).astype(jnp.bfloat16)
    u_terms = lax.dot_general(normed.astype(jnp.float32), t, (((0,), (0,)), ((), ())), precision=HI)
    summed = lax.psum_scatter(terms, "tm", scatter_dimension=0, tiled=True)
    qk_grad = lax.psum(summed, "env").astype(jnp.float32)
    u_mine = lax.psum(u_terms, ("env", "tm"))
    u_mine = lax.dynamic_slice_in_dim(u_mine, lax.axis_index("tm") * w_v.shape[0], w_v.shape[0], 0)
    u_wide = jnp.repeat(u_mine, size, axis=1)
    v_grad = u_wide * v
    mixed_err = lax.psum(jnp.sum(u_wide * w_v, axis=0), "tm")
    mixed_err = lax.dynamic_slice_in_dim(
        mixed_err, lax.axis_index("tm") * w_out_a.shape[0], w_out_a.shape[0], 0
    )
    out_grad = mixed_err[:, None] * w_value
    qkv_grad = jnp.concatenate([qk_grad, v_grad], axis=1)
    input_grad = pull(returned[0])[0]
    return (predicted[None], input_grad[None, None], qkv_grad, out_grad)


def solution(mesh):
    in_specs = (
        P("env", "tm", None, None),
        P("env", "tm"),
        P("env", None, "tm"),
        P("env", None, "tm"),
        P(),
        P(),
        P(),
        P(),
        P("tm", None),
        P("tm", None),
        P(),
    )
    out_specs = (P("env", None, "tm"), P("env", "tm", None, None), P("tm", None), P("tm", None))
    return jax.shard_map(
        per_device, mesh=mesh, in_specs=in_specs, out_specs=out_specs, check_vma=False
    )
```

profile of v0, /device:TPU:1, one launch (start us, length us, event | category | flops | bytes accessed | tf_op | source)
XLA Modules:
  0.0 856.8 jit_solution(7488116643575696525)
XLA Ops:
  7.2 1.6 slice.24
  9.5 1.2 fusion.49
  10.7 0.5 copy-done.25
  11.3 4.9 convolution_convert_fusion
  16.1 1.1 slice_bitcast_fusion
  17.2 1.4 copy.98
  18.7 2.2 copy.97
  21.0 1.6 fusion.114
  23.3 0.7 copy-done.1
  24.0 1.0 copy-done.3
  25.4 0.7 fusion.37
  26.1 0.8 copy.135
  27.0 0.5 broadcast.202
  27.5 4.5 reduce.4
  32.0 2.2 reshape.279
  34.2 15.1 %all-to-all-start = ((bf16[64,2,2048]{2,1,0:T(2,128)(2,1)}), bf16[64,2,2048]{2,1,0:T(2,128)(2,1)S(1)}, u32[]{:S(2)}, u32[]{:S(2)}) async-start(bf16[64,2,2048]{2,1,0:T(2,128)(2,1)} %reshape.279), calls=%async_computation | async-start | bytes 1048576 | tf_op jit(solution)/shard_map/all_to_all | solution.py:102
  49.4 0.6 dynamic-slice
  51.0 156.9 %all-reduce.3 = f32[1024]{0:T(1024)S(1)} all-reduce(f32[1024]{0:T(1024)S(1)} %dynamic-update-slice), channel_id=1, replica_groups=mesh['env'=4,'tm'=64] {'tm'}, use_global_device_ids=true, to_apply=%add.3 | all-reduce | flops 1024 | bytes 8192
  207.9 0.8 fusion.93
  208.9 148.0 %all-gather = f32[64,16,8]{1,2,0:T(8,128)S(1)} all-gather(f32[1,16,8]{1,2,0:T(8,128)S(1)} %bitcast.169), channel_id=1, replica_groups=mesh['env'=4,'tm'=64] {'tm'}, dimensions={0}, use_global_device_ids=true | all-gather | bytes 33280 | tf_op jit(solution)/shard_map/all_gather | solution.py:97
  357.2 0.7 broadcast_or_fusion
  357.9 1.8 reshape.280
  359.7 1.6 fusion.39
  361.5 0.7 copy.75
  362.2 1.3 reshape.268
  363.5 1.5 multiply_convert_fusion
  365.0 0.8 copy-done.6
  365.8 1.3 convolution_bitcast_fusion.3
  367.1 3.5 fusion.16
  370.9 1.0 fusion.113
  371.9 3.5 multiply_reduce_fusion.2
  375.4 1.3 fusion.95
  376.7 3.3 convolution_bitcast_fusion
  380.0 3.4 convolution_bitcast_fusion.1
  383.5 1.3 maximum_convert_fusion
  384.8 1.7 copy.78
  386.4 2.3 convert_element_type.173
  388.7 4.6 convolution_convert_fusion.1
  393.5 0.5 copy-done.22
  394.1 1.6 multiply_reduce_fusion
  395.8 3.8 fusion.115
  399.6 2.1 fusion.40
  401.8 2.6 reshape.260
  404.4 2.8 fusion.47
  407.2 4.9 all-to-all-start.1
  412.1 1.5 convolution_bitcast_fusion.2
  413.6 132.2 %psum.22 = f32[1024,8]{0,1:T(8,128)S(1)} all-reduce(f32[1024,8]{0,1:T(8,128)S(1)} %convolution_bitcast_fusion.2), channel_id=1, replica_groups=mesh['env'=4,'tm'=64] {'env','tm'}, use_global_device_ids=true, to_apply=%region_19.20 | all-reduce | flops 8192 | bytes 65536 | tf_op jit(solution)/shard_map/psum | solution.py:111
  546.0 0.8 fusion.94
  546.8 156.0 %psum.23 = f32[1024]{0:T(1024)S(1)} all-reduce(f32[1024]{0:T(1024)S(1)} %get-tuple-element.19), channel_id=1, replica_groups=mesh['env'=4,'tm'=64] {'tm'}, use_global_device_ids=true, to_apply=%region_21.22 | all-reduce | flops 1024 | bytes 8192 | tf_op jit(solution)/shard_map/psum | solution.py:115
  702.9 0.7 broadcast_multiply_fusion
  703.6 0.9 squeeze.21
  704.6 2.6 convolution_convert_fusion.5
  707.2 1.2 copy.94
  708.5 2.3 fusion.6
  710.9 1.0 convert_reduce_fusion
  712.6 1.2 fusion.25
  713.8 1.2 fusion.24
  715.2 0.7 slice-done.1
  716.0 2.9 fusion.52
  718.9 45.1 %reduce-scatter.2.cloned.1.call-done = bf16[16,2048]{1,0:T(8,128)(2,1)} async-done(((bf16[1024,2048]{1,0:T(8,128)(2,1)}), bf16[16,2048]{1,0:T(8,128)(2,1)}) %reduce-scatter.2.cloned.1.call-update) | async-done | bytes 65552 | tf_op jit(solution)/shard_map/reduce_scatter | solution.py:109
  764.1 2.3 fusion.67
  766.4 82.4 %all-reduce.6.cloned.1.call-done = bf16[16,2048]{1,0:T(8,128)(2,1)} async-done(((bf16[16,2048]{1,0:T(8,128)(2,1)}), bf16[16,2048]{1,0:T(8,128)(2,1)}) %all-reduce.6.cloned.1.call-update) | async-done | bytes 65552 | tf_op jit(solution)/shard_map/psum | solution.py:110
  848.8 0.8 convert_element_type.192
  849.6 0.7 pad_maximum_fusion
  (107 shorter events, 4.4 us)
Async XLA Ops:
  7.2 18.2 %copy-start = (bf16[1024,1024]{1,0:T(8,128)(2,1)S(1)}, bf16[1024,1024]{1,0:T(8,128)(2,1)}, u32[]{:S(2)}) copy-start(bf16[1024,1024]{1,0:T(8,128)(2,1)} %param.17) | copy-start | bytes 6291460
  7.2 359.9 %all-gather.3.cloned.1.call-start = ((), (), s32[]{:S(2)}) async-start(), calls=%async_computation.3 | async-start | bytes 4259840 | tf_op jit(solution)/shard_map/all_gather | solution.py:98
  10.7 0.5 copy-start.25
  11.3 4.9 copy-start.28
  17.2 6.8 copy-start.9
  18.7 3.9 copy-start.11
  22.6 1.4 copy-start.1
  22.9 2.4 copy-start.16
  22.9 2.4 copy-start.7
  24.0 1.0 copy-start.3
  26.9 22.4 %copy-start.31 = (u32[256]{0:T(256)S(1)}, u32[256]{0:T(256)}, u32[]{:S(2)}) copy-start(u32[256]{0:T(256)} %constant.61) | copy-start | bytes 3076
  26.9 23.7 %copy-start.18 = (f32[1024]{0:T(1024)S(1)}, f32[1024]{0:T(1024)}, u32[]{:S(2)}) copy-start(f32[1024]{0:T(1024)} %param.21) | copy-start | bytes 12292
  27.0 23.7 %copy-start.21 = (bf16[16,1024]{1,0:T(8,128)(2,1)S(1)}, bf16[16,1024]{1,0:T(8,128)(2,1)}, u32[]{:S(2)}) copy-start(bf16[16,1024]{1,0:T(8,128)(2,1)} %param.20) | copy-start | bytes 98308
  32.0 325.1 %copy-start.27 = (s32[1,64,4]{1,2,0:T(4,128)S(1)}, s32[1,64,4]{1,2,0:T(4,128)}, u32[]{:S(2)}) copy-start(s32[1,64,4]{1,2,0:T(4,128)} %param.13) | copy-start | bytes 3076
  34.2 323.7 %all-to-all-start = ((bf16[64,2,2048]{2,1,0:T(2,128)(2,1)}), bf16[64,2,2048]{2,1,0:T(2,128)(2,1)S(1)}, u32[]{:S(2)}, u32[]{:S(2)}) async-start(bf16[64,2,2048]{2,1,0:T(2,128)(2,1)} %reshape.279), calls=%async_computation | async-start | bytes 1048576 | tf_op jit(solution)/shard_map/all_to_all | solution.py:102
  49.3 714.7 %reduce-scatter.2.cloned.1.call-start = ((), (), s32[]{:S(2)}) async-start(), calls=%async_computation.4 | async-start | bytes 4259840 | tf_op jit(solution)/shard_map/reduce_scatter | solution.py:109
  207.9 149.2 %copy-start.19 = (f32[1024]{0:T(1024)}, f32[1024]{0:T(1024)S(1)}, u32[]{:S(2)}) copy-start(f32[1024]{0:T(1024)S(1)} %all-reduce.3) | copy-start | bytes 12292
  357.9 5.6 copy-start.15
  361.3 9.4 %copy-start.23 = (f32[256]{0:T(256)}, f32[256]{0:T(256)S(1)}, u32[]{:S(2)}) copy-start(f32[256]{0:T(256)S(1)} %get-tuple-element.24) | copy-start | bytes 3076
  365.0 0.8 copy-start.6
  384.8 4.0 copy-start.24
  393.3 0.7 copy-start.22
  401.7 2.7 copy-start.5
  404.4 7.7 copy-start.17
  404.4 141.6 %copy-start.20 = (f32[1024]{0:T(1024)S(1)}, f32[1024]{0:T(1024)}, u32[]{:S(2)}) copy-start(f32[1024]{0:T(1024)} %copy-done.19) | copy-start | bytes 12292
  407.2 296.4 %all-to-all-start.1 = ((bf16[64,4,1024]{2,1,0:T(4,128)(2,1)}), bf16[64,4,1024]{2,1,0:T(4,128)(2,1)S(1)}, u32[]{:S(2)}, u32[]{:S(2)}) async-start(bf16[64,4,1024]{2,1,0:T(4,128)(2,1)} %fusion.47), calls=%async_computation.1 | async-start | bytes 1048576 | tf_op jit(solution)/shard_map/all_to_all | solution.py:106
  412.0 436.7 %all-reduce.6.cloned.1.call-start = ((), (), s32[]{:S(2)}) async-start(), calls=%async_computation.5 | async-start | bytes 131072 | tf_op jit(solution)/shard_map/psum | solution.py:110
  704.6 3.9 copy-start.10
  708.5 2.4 copy-start.2
  710.8 1.2 copy-start.4
  710.8 1.7 copy-start.12
  712.5 1.2 copy-start.13
  712.5 2.4 slice-start
  713.8 1.5 copy-start.8
  713.8 2.2 slice-start.1
  713.8 2.2 copy-start.30
  716.0 2.9 copy-start.26
  716.0 48.0 %copy-start.14 = (bf16[256,1024]{1,0:T(8,128)(2,1)S(1)}, bf16[256,1024]{1,0:T(8,128)(2,1)}, u32[]{:S(2)}) copy-start(bf16[256,1024]{1,0:T(8,128)(2,1)} %squeeze.21) | copy-start | bytes 1572868
  716.0 48.0 %copy-start.29 = (f32[256]{0:T(256)S(1)}, f32[256]{0:T(256)}, u32[]{:S(2)}) copy-start(f32[256]{0:T(256)} %copy-done.28) | copy-start | bytes 3076
Sparse Core Ops, SparseCore 0:
  12.1 128.8 all-gather.2
  393.4 370.5 reduce-scatter.1
  766.8 81.8 all-reduce.5
where the time goes:
time: 858 us; the launch traced here: 857 us
  blocking collectives  593 us (69%)
  waiting for transfers between devices  128 us (15%)
  matrix products  45.3 us (5%)
  local copies, waits for them, and re-layouts  30.5 us (4%)
  other arithmetic  24.6 us (3%)
  starting transfers between devices  20.1 us (2%)
  between operations  15.7 us (2%)
    unnamed x1, blocking collectives  157 us
    psum x1, blocking collectives, per_device(): mixed_err = lax.psum(jnp.sum(u_wide * w_v, axis=0), 'tm')  156 us
    all_gather x1, blocking collectives, per_device(): z = lax.all_gather(z, 'tm', axis=0, tiled=True)  148 us
    psum x1, blocking collectives, per_device(): u_mine = lax.psum(u_terms, ('env', 'tm'))  132 us
    psum x1, waiting for transfers between devices, per_device(): qk_grad = lax.psum(summed, 'env').astype(jnp.float32)  82.4 us
    reduce_scatter x1, waiting for transfers between devices, per_device(): summed = lax.psum_scatter(terms, 'tm', scatter_dimension=0, tiled=True)  45.1 us
  transfers between devices with their start and end apart: 5, of which 2 were waited for; matrix products, arithmetic and copies ran while one was open for 8% of the time, Pallas kernels for 0%

commit v1 on v0

--- a/solution.py
+++ b/solution.py
@@ -107,7 +107,7 @@
     terms = left_product(normed, dqk).astype(jnp.bfloat16)
     u_terms = lax.dot_general(normed.astype(jnp.float32), t, (((0,), (0,)), ((), ())), precision=HI)
     summed = lax.psum_scatter(terms, "tm", scatter_dimension=0, tiled=True)
-    qk_grad = lax.psum(summed, "env").astype(jnp.float32)
+    qk_grad = jnp.sum(lax.all_gather(summed, "env"), axis=0).astype(jnp.float32)
     u_mine = lax.psum(u_terms, ("env", "tm"))
     u_mine = lax.dynamic_slice_in_dim(u_mine, lax.axis_index("tm") * w_v.shape[0], w_v.shape[0], 0)
     u_wide = jnp.repeat(u_mine, size, axis=1)

time: 858 us -> 828 us (0.965)
  waiting for transfers between devices: 128 us -> 45.1 us
  blocking collectives: 593 us -> 648 us
    psum x1 -> x0, waiting for transfers between devices: 82.4 us -> none  [per_device(): qk_grad = lax.psum(summed, 'env').astype(jnp.float32)]
    all_gather x0 -> x1, blocking collectives: none -> 55 us  [per_device(): qk_grad = jnp.sum(lax.all_gather(summed, 'env'), axis=0).astype(jnp.float32)]
  transfers between devices with their start and end apart: 5 -> 4, of which waited for: 2 -> 1; matrix products, arithmetic and copies ran while one was open for 8% -> 8% of each run, Pallas kernels for 0% -> 0%
where the time goes in v1:
time: 828 us; the launch traced here: 826 us
  blocking collectives  648 us (78%)
  waiting for transfers between devices  45.1 us (5%)
  matrix products  44.4 us (5%)
  local copies, waits for them, and re-layouts  30.4 us (4%)
  other arithmetic  22.6 us (3%)
  starting transfers between devices  20.1 us (2%)
  between operations  16 us (2%)
    unnamed x1, blocking collectives  157 us
    psum x1, blocking collectives, per_device(): mixed_err = lax.psum(jnp.sum(u_wide * w_v, axis=0), 'tm')  155 us
    all_gather x1, blocking collectives, per_device(): z = lax.all_gather(z, 'tm', axis=0, tiled=True)  148 us
    psum x1, blocking collectives, per_device(): u_mine = lax.psum(u_terms, ('env', 'tm'))  132 us
    all_gather x1, blocking collectives, per_device(): qk_grad = jnp.sum(lax.all_gather(summed, 'env'), axis=0).astype(jnp.float32)  55 us
    reduce_scatter x1, waiting for transfers between devices, per_device(): summed = lax.psum_scatter(terms, 'tm', scatter_dimension=0, tiled=True)  45.1 us
  transfers between devices with their start and end apart: 4, of which 1 were waited for; matrix products, arithmetic and copies ran while one was open for 8% of the time, Pallas kernels for 0%

profile of v1, /device:TPU:1, one launch (start us, length us, event | category | flops | bytes accessed | tf_op | source)
XLA Modules:
  0.0 826.2 jit_solution(10811044870625928464)
XLA Ops:
  7.2 1.6 slice.24
  9.5 1.2 fusion.49
  10.7 0.5 copy-done.25
  11.3 4.9 convolution_convert_fusion
  16.1 1.1 slice_bitcast_fusion
  17.2 1.4 copy.98
  18.7 2.2 copy.97
  21.0 1.6 fusion.114
  23.3 0.7 copy-done.1
  24.0 1.0 copy-done.3
  25.4 0.7 fusion.37
  26.1 0.8 copy.135
  27.0 0.5 broadcast.202
  27.5 4.5 reduce.5
  32.0 2.2 reshape.280
  34.2 15.1 %all-to-all-start = ((bf16[64,2,2048]{2,1,0:T(2,128)(2,1)}), bf16[64,2,2048]{2,1,0:T(2,128)(2,1)S(1)}, u32[]{:S(2)}, u32[]{:S(2)}) async-start(bf16[64,2,2048]{2,1,0:T(2,128)(2,1)} %reshape.280), calls=%async_computation | async-start | bytes 1048576 | tf_op jit(solution)/shard_map/all_to_all | solution.py:102
  49.4 0.6 dynamic-slice
  51.0 156.9 %all-reduce.3 = f32[1024]{0:T(1024)S(1)} all-reduce(f32[1024]{0:T(1024)S(1)} %dynamic-update-slice), channel_id=1, replica_groups=mesh['env'=4,'tm'=64] {'tm'}, use_global_device_ids=true, to_apply=%add.3 | all-reduce | flops 1024 | bytes 8192
  207.9 0.8 fusion.93
  208.9 148.0 %all-gather.1 = f32[64,16,8]{1,2,0:T(8,128)S(1)} all-gather(f32[1,16,8]{1,2,0:T(8,128)S(1)} %bitcast.171), channel_id=1, replica_groups=mesh['env'=4,'tm'=64] {'tm'}, dimensions={0}, use_global_device_ids=true | all-gather | bytes 33280 | tf_op jit(solution)/shard_map/all_gather | solution.py:97
  357.2 0.7 broadcast_or_fusion
  357.9 1.8 reshape.281
  359.7 1.6 fusion.39
  361.5 0.7 copy.75
  362.2 1.3 reshape.268
  363.5 1.5 multiply_convert_fusion
  365.0 0.8 copy-done.6
  365.8 1.3 convolution_bitcast_fusion.3
  367.1 3.5 fusion.16
  370.9 1.0 fusion.113
  371.9 3.5 multiply_reduce_fusion.2
  375.4 1.3 fusion.95
  376.7 3.3 convolution_bitcast_fusion
  380.0 3.4 convolution_bitcast_fusion.1
  383.5 1.3 maximum_convert_fusion
  384.8 1.7 copy.78
  386.4 2.3 convert_element_type.175
  388.7 4.6 convolution_convert_fusion.1
  393.5 0.5 copy-done.22
  394.1 1.6 multiply_reduce_fusion
  395.8 3.8 fusion.115
  399.6 2.1 fusion.40
  401.8 2.6 reshape.260
  404.4 2.8 fusion.47
  407.2 4.9 all-to-all-start.1
  412.1 1.5 convolution_bitcast_fusion.2
  413.5 132.3 %psum.14 = f32[1024,8]{0,1:T(8,128)S(1)} all-reduce(f32[1024,8]{0,1:T(8,128)S(1)} %convolution_bitcast_fusion.2), channel_id=1, replica_groups=mesh['env'=4,'tm'=64] {'env','tm'}, use_global_device_ids=true, to_apply=%region_19.20 | all-reduce | flops 8192 | bytes 65536 | tf_op jit(solution)/shard_map/psum | solution.py:111
  546.0 0.8 fusion.94
  546.8 155.3 %psum.15 = f32[1024]{0:T(1024)S(1)} all-reduce(f32[1024]{0:T(1024)S(1)} %get-tuple-element.19), channel_id=1, replica_groups=mesh['env'=4,'tm'=64] {'tm'}, use_global_device_ids=true, to_apply=%region_21.22 | all-reduce | flops 1024 | bytes 8192 | tf_op jit(solution)/shard_map/psum | solution.py:115
  702.2 0.7 broadcast_multiply_fusion
  702.9 0.9 squeeze.21
  703.9 2.7 convolution_convert_fusion.5
  706.5 1.2 copy.94
  707.8 2.3 fusion.6
  710.2 1.0 convert_reduce_fusion
  711.4 0.5 convolution_convert_fusion.4
  711.9 1.2 fusion.25
  713.1 1.2 fusion.24
  714.6 0.7 slice-done.1
  715.3 2.0 fusion.52
  717.3 1.1 fusion.67
  718.5 45.1 %reduce-scatter.2.cloned.1.call-done = bf16[16,2048]{1,0:T(8,128)(2,1)} async-done(((bf16[1024,2048]{1,0:T(8,128)(2,1)}), bf16[16,2048]{1,0:T(8,128)(2,1)}) %reduce-scatter.2.cloned.1.call-update) | async-done | bytes 65552 | tf_op jit(solution)/shard_map/reduce_scatter | solution.py:109
  763.6 55.0 %all-gather = bf16[64,2048]{1,0:T(8,128)(2,1)S(1)} all-gather(bf16[16,2048]{1,0:T(8,128)(2,1)} %reduce-scatter.2.cloned.1.call-done), channel_id=2, replica_groups=mesh['env'=4,'tm'=64] {'env'}, dimensions={0}, use_global_device_ids=true | all-gather | bytes 327680 | tf_op jit(solution)/shard_map/all_gather | solution.py:110
  818.7 0.7 pad_maximum_fusion
  (106 shorter events, 3.9 us)
Async XLA Ops:
  7.2 18.2 %copy-start = (bf16[1024,1024]{1,0:T(8,128)(2,1)S(1)}, bf16[1024,1024]{1,0:T(8,128)(2,1)}, u32[]{:S(2)}) copy-start(bf16[1024,1024]{1,0:T(8,128)(2,1)} %param.17) | copy-start | bytes 6291460
  7.2 359.9 %all-gather.4.cloned.1.call-start = ((), (), s32[]{:S(2)}) async-start(), calls=%async_computation.3 | async-start | bytes 4259840 | tf_op jit(solution)/shard_map/all_gather | solution.py:98
  10.7 0.5 copy-start.25
  11.3 4.9 copy-start.28
  17.2 6.8 copy-start.9
  18.7 3.9 copy-start.11
  22.6 1.4 copy-start.1
  22.9 2.4 copy-start.16
  22.9 2.4 copy-start.7
  24.0 1.0 copy-start.3
  26.9 22.4 %copy-start.31 = (u32[256]{0:T(256)S(1)}, u32[256]{0:T(256)}, u32[]{:S(2)}) copy-start(u32[256]{0:T(256)} %constant.62) | copy-start | bytes 3076
  26.9 23.7 %copy-start.18 = (f32[1024]{0:T(1024)S(1)}, f32[1024]{0:T(1024)}, u32[]{:S(2)}) copy-start(f32[1024]{0:T(1024)} %param.21) | copy-start | bytes 12292
  27.0 23.7 %copy-start.21 = (bf16[16,1024]{1,0:T(8,128)(2,1)S(1)}, bf16[16,1024]{1,0:T(8,128)(2,1)}, u32[]{:S(2)}) copy-start(bf16[16,1024]{1,0:T(8,128)(2,1)} %param.20) | copy-start | bytes 98308
  32.0 325.1 %copy-start.27 = (s32[1,64,4]{1,2,0:T(4,128)S(1)}, s32[1,64,4]{1,2,0:T(4,128)}, u32[]{:S(2)}) copy-start(s32[1,64,4]{1,2,0:T(4,128)} %param.13) | copy-start | bytes 3076
  34.2 323.7 %all-to-all-start = ((bf16[64,2,2048]{2,1,0:T(2,128)(2,1)}), bf16[64,2,2048]{2,1,0:T(2,128)(2,1)S(1)}, u32[]{:S(2)}, u32[]{:S(2)}) async-start(bf16[64,2,2048]{2,1,0:T(2,128)(2,1)} %reshape.280), calls=%async_computation | async-start | bytes 1048576 | tf_op jit(solution)/shard_map/all_to_all | solution.py:102
  49.3 714.3 %reduce-scatter.2.cloned.1.call-start = ((), (), s32[]{:S(2)}) async-start(), calls=%async_computation.4 | async-start | bytes 4259840 | tf_op jit(solution)/shard_map/reduce_scatter | solution.py:109
  207.9 149.2 %copy-start.19 = (f32[1024]{0:T(1024)}, f32[1024]{0:T(1024)S(1)}, u32[]{:S(2)}) copy-start(f32[1024]{0:T(1024)S(1)} %all-reduce.3) | copy-start | bytes 12292
  357.9 5.6 copy-start.15
  361.3 9.4 %copy-start.23 = (f32[256]{0:T(256)}, f32[256]{0:T(256)S(1)}, u32[]{:S(2)}) copy-start(f32[256]{0:T(256)S(1)} %get-tuple-element.24) | copy-start | bytes 3076
  365.0 0.8 copy-start.6
  384.8 4.0 copy-start.24
  393.3 0.7 copy-start.22
  401.7 2.7 copy-start.5
  404.4 7.7 copy-start.17
  404.4 141.6 %copy-start.20 = (f32[1024]{0:T(1024)S(1)}, f32[1024]{0:T(1024)}, u32[]{:S(2)}) copy-start(f32[1024]{0:T(1024)} %copy-done.19) | copy-start | bytes 12292
  407.2 295.8 %all-to-all-start.1 = ((bf16[64,4,1024]{2,1,0:T(4,128)(2,1)}), bf16[64,4,1024]{2,1,0:T(4,128)(2,1)S(1)}, u32[]{:S(2)}, u32[]{:S(2)}) async-start(bf16[64,4,1024]{2,1,0:T(4,128)(2,1)} %fusion.47), calls=%async_computation.1 | async-start | bytes 1048576 | tf_op jit(solution)/shard_map/all_to_all | solution.py:106
  703.9 3.9 copy-start.10
  707.8 2.4 copy-start.2
  710.1 1.2 copy-start.4
  710.2 1.7 copy-start.12
  711.9 1.2 copy-start.13
  711.9 2.4 slice-start
  713.1 1.5 copy-start.8
  713.1 2.2 slice-start.1
  713.1 2.2 copy-start.30
  715.3 2.0 copy-start.26
  715.3 2.0 copy-start.14
  715.3 2.0 copy-start.29
Sparse Core Ops, SparseCore 0:
  12.1 128.8 all-gather.3
  393.4 370.0 reduce-scatter.1
